TPU v7x, 256 devices: a whole 4x4x8 slice. The times are simulated.
256 devices in a mesh: dp: 8 (over y, core), expert: 32 (over z, x).
Axes of the slice: x: 4, y: 4, z: 8, core: 2. Of those that a mesh axis runs over, the one named last changes fastest.
Arguments:
- tokens: bfloat16 [4096, 7168], P('expert', 'dp'), may hold values from -6 to 6
- cotangent: bfloat16 [4096, 7168], P('expert', 'dp'), may hold values from -6 to 6
- expert_ids: int32 [4096, 8], P('expert'), may hold values from 0 to 31, all different within a row; in each aligned block of 128 rows (0 to 127, 128 to 255, ...) at most 40 rows name the same one
- gates: float32 [4096, 8], P('expert'), may hold values from 0.05 to 0.5
- up_weight: bfloat16 [32, 7168, 1024], P('expert', 'dp'), may hold values from -0.0625 to 0.0625
- down_weight: bfloat16 [32, 1024, 7168], P('expert', None, 'dp'), may hold values from -0.1875 to 0.1875
Outputs:
- mixed: bfloat16 [4096, 7168], P('expert', 'dp')
- input_grads: bfloat16 [4096, 7168], P('expert', 'dp')
- up_grads: bfloat16 [32, 7168, 1024], P('expert', 'dp')
- down_grads: bfloat16 [32, 1024, 7168], P('expert', None, 'dp')
- gate_grads: float32 [4096, 8], P('expert')
Inputs may be any that keep to these rules, and one draw needn't show every extreme that they name: `expert_ids`: each row names 8 different experts. In the rows of one index of the expert axis no expert is named by more than 40 rows, a bound that some block reaches of them.
All inputs are finite; a program needn't handle non-finite values.
Results may differ from a plain program's by a relative error of at most 0.0064.
Values may be sent and summed in bfloat16 or wider, within the bound.
No kernel may reach another device: no remote copies, remote signals or barrier semaphores. Data moves between devices by JAX's collectives and lax.ppermute only.
A program may use at most 128 MiB of HBM per device.

v0:
```python
import jax
import jax.numpy as jnp
from jax import lax
from jax.sharding import PartitionSpec as P


def silu_slope(preact):
    logistic = jax.nn.sigmoid(preact)
    return logistic * (1.0 + preact * (1.0 - logistic))


def per_device(tokens, cotangent, expert_ids, gates, up_weight, down_weight):
    tok_count = tokens.shape[0]
    width_part = tokens.shape[1]
    top_count = expert_ids.shape[1]
    experts = lax.axis_size("expert")
    capacity = tok_count * top_count * 5 // (4 * experts)
    slot_total = experts * capacity
    replicas = lax.axis_size("dp")
    share_rows = slot_total // replicas
    first_row = lax.axis_index("dp") * share_rows
    flat_ids = expert_ids.reshape(-1)
    labels = jnp.arange(experts, dtype=jnp.int32)
    chosen = (flat_ids[:, None] == labels[None, :]).astype(jnp.int32)
    before = jnp.cumsum(chosen, axis=0) - chosen
    position = jnp.sum(before * chosen, axis=1)
    slot_index = flat_ids * capacity + position
    token_rows = jnp.repeat(tokens, top_count, axis=0)
    scaled_rows = (
        gates.reshape(-1, 1) * jnp.repeat(cotangent, top_count, axis=0).astype(jnp.float32)
    ).astype(jnp.bfloat16)
    empty_buffer = jnp.zeros((slot_total, width_part), jnp.bfloat16)
    send_tokens = empty_buffer.at[slot_index].set(token_rows).reshape(experts, capacity, width_part)
    send_scaled = (
        empty_buffer.at[slot_index].set(scaled_rows).reshape(experts, capacity, width_part)
    )
    recv_tokens, recv_scaled = (
        lax.all_to_all(send_tokens, "expert", split_axis=0, concat_axis=0, tiled=True),
        lax.all_to_all(send_scaled, "expert", split_axis=0, concat_axis=0, tiled=True),
    )
    x_slots = recv_tokens.reshape(slot_total, width_part)
    g_slots = recv_scaled.reshape(slot_total, width_part)
    w_up = up_weight[0]
    w_down = down_weight[0]
    preact = lax.psum(jnp.dot(x_slots, w_up, preferred_element_type=jnp.float32), "dp")
    hidden = jax.nn.silu(preact).astype(jnp.bfloat16)
    preact_share = lax.dynamic_slice_in_dim(preact, first_row, share_rows, 0)
    out_slots = jnp.dot(hidden, w_down, preferred_element_type=jnp.float32).astype(jnp.bfloat16)
    out_send = out_slots.reshape(experts, capacity, width_part)
    back_out = lax.all_to_all(out_send, "expert", split_axis=0, concat_axis=0, tiled=True)
    hidden_grad = lax.psum_scatter(
        lax.dot_general(
            g_slots, w_down, (((1,), (1,)), ((), ())), preferred_element_type=jnp.float32
        ),
        "dp",
        scatter_dimension=0,
        tiled=True,
    )
    grad_share = (hidden_grad * silu_slope(preact_share)).astype(jnp.bfloat16)
    preact_grad = lax.all_gather(grad_share, "dp", axis=0, tiled=True)
    slot_dx = lax.dot_general(
        preact_grad, w_up, (((1,), (1,)), ((), ())), preferred_element_type=jnp.float32
    ).astype(jnp.bfloat16)
    dx_send = slot_dx.reshape(experts, capacity, width_part)
    back_dx = lax.all_to_all(dx_send, "expert", split_axis=0, concat_axis=0, tiled=True)
    down_grad = lax.dot_general(
        hidden, g_slots, (((0,), (0,)), ((), ())), preferred_element_type=jnp.float32
    ).astype(jnp.bfloat16)
    up_grad = lax.dot_general(
        x_slots, preact_grad, (((0,), (0,)), ((), ())), preferred_element_type=jnp.float32
    ).astype(jnp.bfloat16)
    expert_out = (
        back_out.reshape(slot_total, width_part)[slot_index]
        .reshape(tok_count, top_count, width_part)
        .astype(jnp.float32)
    )
    mixed = jnp.sum(gates[:, :, None] * expert_out, axis=1).astype(jnp.bfloat16)
    gate_terms = jnp.sum(cotangent[:, None, :].astype(jnp.float32) * expert_out, axis=2)
    gate_grads = lax.psum(gate_terms, "dp")
    dx_rows = (
        back_dx.reshape(slot_total, width_part)[slot_index]
        .reshape(tok_count, top_count, width_part)
        .astype(jnp.float32)
    )
    input_grads = jnp.sum(dx_rows, axis=1).astype(jnp.bfloat16)
    return (mixed, input_grads, up_grad[None], down_grad[None], gate_grads)


def solution(mesh):
    placed = (
        P("expert", "dp"),
        P("expert", "dp"),
        P("expert", None),
        P("expert", None),
        P("expert", "dp", None),
        P("expert", None, "dp"),
    )
    return jax.shard_map(
        per_device,
        mesh=mesh,
        in_specs=placed,
        out_specs=(
            P("expert", "dp"),
            P("expert", "dp"),
            P("expert", "dp", None),
            P("expert", None, "dp"),
            P("expert", None),
        ),
        check_vma=False,
    )
```

profile of v0, /device:TPU:24, one launch (start us, length us, event | category | flops | bytes accessed | tf_op | source)
XLA Modules:
  0.0 383.9 jit_solution(936221111414959934)
XLA Ops:
  7.2 0.0 copy-start
  7.2 0.8 broadcast_multiply_fusion
  8.0 0.8 copy.21
  8.8 0.1 eq.29
  8.9 0.1 eq.25
  9.0 0.1 copy.20
  9.1 0.1 mul.66
  9.2 9.0 %reduce-window.6 = s32[32,8,128]{2,1,0:T(8,128)S(1)} reduce-window(s32[32,8,128]{2,1,0:T(8,128)S(1)} %fusion.21, s32[]{:T(128)} %constant.11.clone.1), window={size=1x1x128 pad=0_0x0_0x127_0}, to_apply=%region_0.0 | reduce-window | flops 4161536 | bytes 262148 | tf_op jit(solution)/shard_map/reduce-window
  18.2 0.1 slice.12
  18.3 0.1 copy.23
  18.5 0.1 copy.24
  18.6 0.1 broadcast_add_fusion
  18.7 7.2 %scatter_custom_fusion = bf16[1280,896]{1,0:T(8,128)(2,1)} fusion(s32[1024]{0:T(1024)S(1)} %bitcast.73, bf16[]{:T(256)} %constant.9.clone.1, bf16[128,896]{1,0:T(8,128)(2,1)} %param.6), kind=kCustom, calls=%fused_computation.21 | custom fusion | bytes 2523138 | tf_op jit(solution)/shard_map/scatter | solution.py:33
  26.0 0.0 copy-start.3
  26.0 0.0 copy-start.2
  26.0 11.6 %all-to-all-start = ((bf16[32,40,896]{2,1,0:T(8,128)(2,1)}), bf16[32,40,896]{2,1,0:T(8,128)(2,1)}, u32[]{:S(2)}, u32[]{:S(2)}) async-start(bf16[32,40,896]{2,1,0:T(8,128)(2,1)} %bitcast.67), calls=%async_computation | async-start | bytes 4587520 | tf_op jit(solution)/shard_map/all_to_all | solution.py:38
  37.5 0.0 copy-done.3
  37.6 0.1 copy.19
  37.7 0.1 mul.70
  37.8 0.0 copy-done.2
  37.8 7.3 %scatter_custom_fusion.1 = bf16[1280,896]{1,0:T(8,128)(2,1)} fusion(s32[1024]{0:T(1024)S(1)} %bitcast.74, f32[128,896]{1,0:T(8,128)S(1)} %convert_element_type.59, f32[1024]{0:T(1024)S(1)} %mul.70, bf16[]{:T(256)} %constant.9.clone.1), kind=kCustom, calls=%fused_computation.13 | custom fusion | flops 1835008 | bytes 2756610 | tf_op jit(solution)/shard_map/scatter | solution.py:35
  45.1 46.8 %all-to-all-done = bf16[32,40,896]{2,1,0:T(8,128)(2,1)} async-done(((bf16[32,40,896]{2,1,0:T(8,128)(2,1)}), bf16[32,40,896]{2,1,0:T(8,128)(2,1)}, u32[]{:S(2)}, u32[]{:S(2)}) %all-to-all-start) | async-done | bytes 2293792 | tf_op jit(solution)/shard_map/all_to_all | solution.py:38
  91.9 5.5 %all-to-all-start.2 = ((bf16[32,40,896]{2,1,0:T(8,128)(2,1)}), bf16[32,40,896]{2,1,0:T(8,128)(2,1)}, u32[]{:S(2)}, u32[]{:S(2)}) async-start(bf16[32,40,896]{2,1,0:T(8,128)(2,1)} %bitcast.66), calls=%async_computation.2 | async-start | bytes 4587520 | tf_op jit(solution)/shard_map/all_to_all | solution.py:39
  97.4 0.0 all-reduce.2.cloned.1.call-start
  97.5 7.4 %fusion.9 = f32[1280,1024]{1,0:T(8,128)} fusion(bf16[1280,896]{1,0:T(8,128)(2,1)} %bitcast.6, bf16[1,896,1024]{2,1,0:T(8,128)(2,1)} %param.10), kind=kOutput, calls=%fused_computation.19 | convolution fusion | flops 2348810240 | bytes 9371648 | tf_op jit(solution)/shard_map/dot_general | solution.py:45
  104.9 0.0 all-reduce.2.cloned.1.call-update
  104.9 0.2 reduce-scatter.2.cloned.1.call-start
  105.1 46.3 %all-to-all-done.2 = bf16[32,40,896]{2,1,0:T(8,128)(2,1)} async-done(((bf16[32,40,896]{2,1,0:T(8,128)(2,1)}), bf16[32,40,896]{2,1,0:T(8,128)(2,1)}, u32[]{:S(2)}, u32[]{:S(2)}) %all-to-all-start.2) | async-done | bytes 2293792 | tf_op jit(solution)/shard_map/all_to_all | solution.py:39
  151.4 0.0 copy-done
  151.4 6.3 %fusion.5 = f32[1280,1024]{1,0:T(8,128)} fusion(bf16[1280,896]{1,0:T(8,128)(2,1)} %bitcast.14, bf16[1,1024,896]{2,1,0:T(8,128)(2,1)S(1)} %copy-done), kind=kOutput, calls=%fused_computation.15 | convolution fusion | flops 2348810240 | bytes 9371648 | tf_op jit(solution)/shard_map/dot_general | solution.py:52
  157.7 0.0 reduce-scatter.2.cloned.1.call-update
  157.7 0.0 all-gather.2.cloned.1.call-start
  157.8 29.1 %all-reduce.2.cloned.1.call-done = f32[1280,1024]{1,0:T(8,128)} async-done(((f32[1280,1024]{1,0:T(8,128)}), f32[1280,1024]{1,0:T(8,128)}) %all-reduce.2.cloned.1.call-update) | async-done | bytes 5242896 | tf_op jit(solution)/shard_map/psum | solution.py:45
  186.8 43.6 %reduce-scatter.2.cloned.1.call-done = f32[160,1024]{1,0:T(8,128)} async-done(((f32[1280,1024]{1,0:T(8,128)}), f32[160,1024]{1,0:T(8,128)}) %reduce-scatter.2.cloned.1.call-update) | async-done | bytes 655376 | tf_op jit(solution)/shard_map/reduce_scatter | solution.py:51
  230.5 2.2 multiply_convert_fusion.1
  232.7 0.0 all-gather.2.cloned.1.call-update
  232.7 3.9 %multiply_convert_fusion = bf16[1280,1024]{1,0:T(8,128)(2,1)S(1)} fusion(f32[1280,1024]{1,0:T(8,128)} %all-reduce.2.cloned.1.call-done), kind=kLoop, calls=%fused_computation.4 | loop fusion | flops 6553600 | bytes 7864320 | tf_op jit(solution)/shard_map/convert_element_type | solution.py:46
  236.6 0.0 copy-start.1
  236.6 4.1 %convolution_convert_fusion.1 = bf16[1280,896]{1,0:T(8,128)(2,1)} fusion(bf16[1280,1024]{1,0:T(8,128)(2,1)S(1)} %multiply_convert_fusion, bf16[1,1024,896]{2,1,0:T(8,128)(2,1)S(1)} %copy-done), kind=kOutput, calls=%fused_computation.12 | convolution fusion | flops 2349957120 | bytes 6750208 | tf_op jit(solution)/shard_map/dot_general | solution.py:48
  240.7 0.0 copy-done.1
  240.7 9.9 %all-to-all-start.1 = ((bf16[32,40,896]{2,1,0:T(8,128)(2,1)}), bf16[32,40,896]{2,1,0:T(8,128)(2,1)}, u32[]{:S(2)}, u32[]{:S(2)}) async-start(bf16[32,40,896]{2,1,0:T(8,128)(2,1)} %bitcast.69), calls=%async_computation.1 | async-start | bytes 4587520 | tf_op jit(solution)/shard_map/all_to_all | solution.py:50
  250.7 13.0 %all-gather.2.cloned.1.call-done = bf16[1280,1024]{1,0:T(8,128)(2,1)} async-done(((bf16[160,1024]{1,0:T(8,128)(2,1)}), bf16[1280,1024]{1,0:T(8,128)(2,1)}) %all-gather.2.cloned.1.call-update) | async-done | bytes 2621456 | tf_op jit(solution)/shard_map/all_gather | solution.py:60
  263.7 6.6 %convolution_convert_fusion = bf16[1280,896]{1,0:T(8,128)(2,1)} fusion(bf16[1280,1024]{1,0:T(8,128)(2,1)} %all-gather.2.cloned.1.call-done, bf16[1,896,1024]{2,1,0:T(8,128)(2,1)} %param.10), kind=kOutput, calls=%fused_computation.11 | convolution fusion | flops 2349957120 | bytes 6750208 | tf_op jit(solution)/shard_map/dot_general | solution.py:61
  270.3 34.5 %all-to-all-done.1 = bf16[32,40,896]{2,1,0:T(8,128)(2,1)} async-done(((bf16[32,40,896]{2,1,0:T(8,128)(2,1)}), bf16[32,40,896]{2,1,0:T(8,128)(2,1)}, u32[]{:S(2)}, u32[]{:S(2)}) %all-to-all-start.1) | async-done | bytes 2293792 | tf_op jit(solution)/shard_map/all_to_all | solution.py:50
  304.8 7.1 %all-to-all-start.3 = ((bf16[32,40,896]{2,1,0:T(8,128)(2,1)}), bf16[32,40,896]{2,1,0:T(8,128)(2,1)}, u32[]{:S(2)}, u32[]{:S(2)}) async-start(bf16[32,40,896]{2,1,0:T(8,128)(2,1)} %bitcast.68), calls=%async_computation.4 | async-start | bytes 4587520 | tf_op jit(solution)/shard_map/all_to_all | solution.py:65
  311.9 6.6 %convert_bitcast_fusion = bf16[1,1024,896]{2,1,0:T(8,128)(2,1)} fusion(bf16[1280,1024]{1,0:T(8,128)(2,1)} %copy-done.1, bf16[1280,896]{1,0:T(8,128)(2,1)} %bitcast.14), kind=kOutput, calls=%fused_computation.23 | convolution fusion | flops 2349727744 | bytes 6750208 | tf_op jit(solution)/shard_map/dot_general | solution.py:66
  318.5 7.7 %gather_fusion = bf16[1024,896]{1,0:T(8,128)(2,1)} fusion(bf16[1280,896]{1,0:T(8,128)(2,1)} %bitcast.10, s32[1024]{0:T(1024)S(1)} %broadcast_clamp_fusion), kind=kCustom, calls=%fused_computation | custom fusion | bytes 3674112 | tf_op jit(solution)/shard_map/gather | solution.py:73
  326.2 3.7 fusion.1
  329.9 24.6 %psum.15 = f32[128,8]{1,0:T(8,128)S(1)} all-reduce(f32[128,8]{1,0:T(8,128)S(1)} %get-tuple-element.10), channel_id=1, replica_groups=mesh['dp'=8,'expert'=32] {'dp'}, use_global_device_ids=true, to_apply=%region_10.11 | all-reduce | flops 1024 | bytes 8192 | tf_op jit(solution)/shard_map/psum | solution.py:79
  354.5 0.7 copy.26
  355.2 6.2 %convert_bitcast_fusion.1 = bf16[1,896,1024]{2,1,0:T(8,128)(2,1)} fusion(bf16[1280,896]{1,0:T(8,128)(2,1)} %bitcast.6, bf16[1280,1024]{1,0:T(8,128)(2,1)} %all-gather.2.cloned.1.call-done), kind=kOutput, calls=%fused_computation.24 | convolution fusion | flops 2349727744 | bytes 6750208 | tf_op jit(solution)/shard_map/dot_general | solution.py:69
  361.4 4.8 %all-to-all-done.3 = bf16[32,40,896]{2,1,0:T(8,128)(2,1)} async-done(((bf16[32,40,896]{2,1,0:T(8,128)(2,1)}), bf16[32,40,896]{2,1,0:T(8,128)(2,1)}, u32[]{:S(2)}, u32[]{:S(2)}) %all-to-all-start.3) | async-done | bytes 2293792 | tf_op jit(solution)/shard_map/all_to_all | solution.py:65
  366.2 7.7 %gather_fusion.1 = bf16[1024,896]{1,0:T(8,128)(2,1)} fusion(bf16[1280,896]{1,0:T(8,128)(2,1)} %bitcast.16, s32[1024]{0:T(1024)S(1)} %broadcast_clamp_fusion), kind=kCustom, calls=%fused_computation.1 | custom fusion | bytes 3674112 | tf_op jit(solution)/shard_map/gather | solution.py:81
  373.9 3.4 bitcast_reduce_fusion
  (7 shorter events, 0.1 us)
Async XLA Ops:
  7.2 144.2 %copy-start = (bf16[1,1024,896]{2,1,0:T(8,128)(2,1)S(1)}, bf16[1,1024,896]{2,1,0:T(8,128)(2,1)}, u32[]{:S(2)}) copy-start(bf16[1,1024,896]{2,1,0:T(8,128)(2,1)} %param.11) | copy-start | bytes 5505028
  26.0 11.6 %copy-start.3 = (f32[128,8]{0,1:T(8,128)S(1)}, f32[128,8]{0,1:T(8,128)}, u32[]{:S(2)}) copy-start(f32[128,8]{0,1:T(8,128)} %param.9) | copy-start | bytes 12292
  26.0 11.8 %copy-start.2 = (bf16[128,896]{1,0:T(8,128)(2,1)S(1)}, bf16[128,896]{1,0:T(8,128)(2,1)}, u32[]{:S(2)}) copy-start(bf16[128,896]{1,0:T(8,128)(2,1)} %param.7) | copy-start | bytes 688132
  26.0 65.9 %all-to-all-start = ((bf16[32,40,896]{2,1,0:T(8,128)(2,1)}), bf16[32,40,896]{2,1,0:T(8,128)(2,1)}, u32[]{:S(2)}, u32[]{:S(2)}) async-start(bf16[32,40,896]{2,1,0:T(8,128)(2,1)} %bitcast.67), calls=%async_computation | async-start | bytes 4587520 | tf_op jit(solution)/shard_map/all_to_all | solution.py:38
  91.9 59.5 %all-to-all-start.2 = ((bf16[32,40,896]{2,1,0:T(8,128)(2,1)}), bf16[32,40,896]{2,1,0:T(8,128)(2,1)}, u32[]{:S(2)}, u32[]{:S(2)}) async-start(bf16[32,40,896]{2,1,0:T(8,128)(2,1)} %bitcast.66), calls=%async_computation.2 | async-start | bytes 4587520 | tf_op jit(solution)/shard_map/all_to_all | solution.py:39
  97.4 89.4 %all-reduce.2.cloned.1.call-start = ((), (), s32[]{:S(2)}) async-start(), calls=%async_computation.5 | async-start | bytes 10485760 | tf_op jit(solution)/shard_map/psum | solution.py:45
  104.9 125.6 %reduce-scatter.2.cloned.1.call-start = ((), (), s32[]{:S(2)}) async-start(), calls=%async_computation.6 | async-start | bytes 5898240 | tf_op jit(solution)/shard_map/reduce_scatter | solution.py:51
  157.7 106.0 %all-gather.2.cloned.1.call-start = ((), (), s32[]{:S(2)}) async-start(), calls=%async_computation.7 | async-start | bytes 2949120 | tf_op jit(solution)/shard_map/all_gather | solution.py:60
  236.6 4.1 %copy-start.1 = (bf16[1280,1024]{1,0:T(8,128)(2,1)}, bf16[1280,1024]{1,0:T(8,128)(2,1)S(1)}, u32[]{:S(2)}) copy-start(bf16[1280,1024]{1,0:T(8,128)(2,1)S(1)} %multiply_convert_fusion) | copy-start | bytes 7864324
  240.7 64.1 %all-to-all-start.1 = ((bf16[32,40,896]{2,1,0:T(8,128)(2,1)}), bf16[32,40,896]{2,1,0:T(8,128)(2,1)}, u32[]{:S(2)}, u32[]{:S(2)}) async-start(bf16[32,40,896]{2,1,0:T(8,128)(2,1)} %bitcast.69), calls=%async_computation.1 | async-start | bytes 4587520 | tf_op jit(solution)/shard_map/all_to_all | solution.py:50
  304.8 61.4 %all-to-all-start.3 = ((bf16[32,40,896]{2,1,0:T(8,128)(2,1)}), bf16[32,40,896]{2,1,0:T(8,128)(2,1)}, u32[]{:S(2)}, u32[]{:S(2)}) async-start(bf16[32,40,896]{2,1,0:T(8,128)(2,1)} %bitcast.68), calls=%async_computation.4 | async-start | bytes 4587520 | tf_op jit(solution)/shard_map/all_to_all | solution.py:65
Sparse Core Ops, SparseCore 0:
  105.0 81.7 all-reduce.1
  189.4 41.0 reduce-scatter.1
  232.9 30.7 all-gather.1
where the time goes:
time: 385 us; the launch traced here: 384 us
  waiting for transfers between devices  218 us (57%)
  matrix products  37.3 us (10%)
  starting transfers between devices  34.4 us (9%)
  other arithmetic  30.6 us (8%)
  local copies, waits for them, and re-layouts  24.9 us (6%)
  blocking collectives  24.6 us (6%)
  between operations  13.9 us (4%)
    all_to_all x1, waiting for transfers between devices, per_device(): lax.all_to_all(send_tokens, 'expert', split_axis=0, concat_axis=0, tiled=...  46.8 us
    all_to_all x1, waiting for transfers between devices, per_device(): lax.all_to_all(send_scaled, 'expert', split_axis=0, concat_axis=0, tiled=...  46.3 us
    reduce_scatter x1, waiting for transfers between devices, per_device(): lax.psum_scatter(lax.dot_general(g_slots, w_down, (((1,), (1,)), ((), ())...  43.6 us
    all_to_all x1, waiting for transfers between devices, per_device(): lax.all_to_all(out_send, 'expert', split_axis=0, concat_axis=0, tiled=True)  34.5 us
    psum x1, waiting for transfers between devices, per_device(): lax.psum(jnp.dot(x_slots, w_up, preferred_element_type=jnp.float32), 'dp')  29.1 us
    psum x1, blocking collectives, per_device(): gate_grads = lax.psum(gate_terms, 'dp')  24.6 us
    all_gather x1, waiting for transfers between devices, per_device(): preact_grad = lax.all_gather(grad_share, 'dp', axis=0, tiled=True)  13 us
    all_to_all x1, starting transfers between devices, per_device(): lax.all_to_all(send_tokens, 'expert', split_axis=0, concat_axis=0, tiled=...  11.6 us
  transfers between devices with their start and end apart: 7, of which 7 were waited for; matrix products, arithmetic and copies ran while one was open for 16% of the time, Pallas kernels for 0%

commit v1 on v0

--- a/solution.py
+++ b/solution.py
@@ -42,7 +42,9 @@
     g_slots = recv_scaled.reshape(slot_total, width_part)
     w_up = up_weight[0]
     w_down = down_weight[0]
-    preact = lax.psum(jnp.dot(x_slots, w_up, preferred_element_type=jnp.float32), "dp")
+    preact = jnp.sum(
+        lax.all_gather(jnp.dot(x_slots, w_up, preferred_element_type=jnp.float32), "dp"), axis=0
+    )
     hidden = jax.nn.silu(preact).astype(jnp.bfloat16)
     preact_share = lax.dynamic_slice_in_dim(preact, first_row, share_rows, 0)
     out_slots = jnp.dot(hidden, w_down, preferred_element_type=jnp.float32).astype(jnp.bfloat16)

time: 385 us -> 485 us (1.26)
  blocking collectives: 24.6 us -> 152 us
  waiting for transfers between devices: 218 us -> 194 us
  other arithmetic: 30.6 us -> 48.6 us
  starting transfers between devices: 34.4 us -> 16.9 us
  matrix products: 37.3 us -> 32.2 us
    all_to_all x0 -> x2, blocking collectives: none -> 128 us  [the longest x1 68 us: per_device(): lax.all_to_all(send_tokens, 'expert', split_axis=0, concat_axis=0, tiled=...]
    all_gather x0 -> x1, waiting for transfers between devices: none -> 114 us  [per_device(): lax.all_gather(jnp.dot(x_slots, w_up, preferred_element_type=jnp.float32)...]
    all_to_all x2 -> x0, waiting for transfers between devices: 93 us -> none  [the longest x1 46.8 us: per_device(): lax.all_to_all(send_tokens, 'expert', split_axis=0, concat_axis=0, tiled=...]
    psum x1 -> x0, waiting for transfers between devices: 29.1 us -> none  [per_device(): lax.psum(jnp.dot(x_slots, w_up, preferred_element_type=jnp.float32), 'dp')]
    reduce_scatter x1, waiting for transfers between devices: 43.6 us -> 24.8 us  [per_device(): lax.psum_scatter(lax.dot_general(g_slots, w_down, (((1,), (1,)), ((), ())...]
    reduce_sum x0 -> x1, other arithmetic: none -> 17.9 us  [per_device(): jnp.sum(lax.all_gather(jnp.dot(x_slots, w_up, preferred_element_type=jnp....]
    all_to_all x2 -> x0, starting transfers between devices: 17.1 us -> none  [the longest x1 11.6 us: per_device(): lax.all_to_all(send_tokens, 'expert', split_axis=0, concat_axis=0, tiled=...]
  transfers between devices with their start and end apart: 7 -> 5, of which waited for: 7 -> 5; matrix products, arithmetic and copies ran while one was open for 16% -> 14% of each run, Pallas kernels for 0% -> 0%
where the time goes in v1:
time: 485 us
  waiting for transfers between devices  194 us (40%)
  blocking collectives  152 us (31%)
  other arithmetic  48.6 us (10%)
  matrix products  32.2 us (7%)
  local copies, waits for them, and re-layouts  26.3 us (5%)
  starting transfers between devices  16.9 us (3%)
  between operations  13.9 us (3%)
    all_gather x1, waiting for transfers between devices, per_device(): lax.all_gather(jnp.dot(x_slots, w_up, preferred_element_type=jnp.float32)...  114 us
    all_to_all x1, blocking collectives, per_device(): lax.all_to_all(send_tokens, 'expert', split_axis=0, concat_axis=0, tiled=...  68 us
    all_to_all x1, blocking collectives, per_device(): lax.all_to_all(send_scaled, 'expert', split_axis=0, concat_axis=0, tiled=...  59.7 us
    all_to_all x1, waiting for transfers between devices, per_device(): lax.all_to_all(out_send, 'expert', split_axis=0, concat_axis=0, tiled=True)  34.4 us
    reduce_scatter x1, waiting for transfers between devices, per_device(): lax.psum_scatter(lax.dot_general(g_slots, w_down, (((1,), (1,)), ((), ())...  24.8 us
    psum x1, blocking collectives, per_device(): gate_grads = lax.psum(gate_terms, 'dp')  24.7 us
    reduce_sum x1, other arithmetic, per_device(): jnp.sum(lax.all_gather(jnp.dot(x_slots, w_up, preferred_element_type=jnp....  17.9 us
    all_gather x1, waiting for transfers between devices, per_device(): preact_grad = lax.all_gather(grad_share, 'dp', axis=0, tiled=True)  13.2 us
  transfers between devices with their start and end apart: 5, of which 5 were waited for; matrix products, arithmetic and copies ran while one was open for 14% of the time, Pallas kernels for 0%

profile of v1, /device:TPU:24, one launch (start us, length us, event | category | flops | bytes accessed | tf_op | source)
XLA Modules:
  0.0 484.8 jit_solution(870534877131174547)
XLA Ops:
  7.2 0.0 copy-start
  7.2 0.0 all-gather.6.cloned.1.call-start
  7.2 0.8 broadcast_multiply_fusion
  8.0 0.8 copy.21
  8.8 0.1 eq.29
  8.9 0.1 eq.25
  9.0 0.1 copy.20
  9.1 0.1 mul.66
  9.2 9.0 %reduce-window.6 = s32[32,8,128]{2,1,0:T(8,128)S(1)} reduce-window(s32[32,8,128]{2,1,0:T(8,128)S(1)} %fusion.21, s32[]{:T(128)} %constant.11.clone.1), window={size=1x1x128 pad=0_0x0_0x127_0}, to_apply=%region_0.0 | reduce-window | flops 4161536 | bytes 262148 | tf_op jit(solution)/shard_map/reduce-window
  18.2 0.1 slice.12
  18.3 0.1 copy.23
  18.5 0.1 copy.24
  18.6 0.1 broadcast_add_fusion
  18.8 7.2 %scatter_custom_fusion = bf16[1280,896]{1,0:T(8,128)(2,1)} fusion(s32[1024]{0:T(1024)S(1)} %bitcast.78, bf16[]{:T(256)} %constant.9.clone.1, bf16[128,896]{1,0:T(8,128)(2,1)} %param.6), kind=kCustom, calls=%fused_computation.21 | custom fusion | bytes 2523138 | tf_op jit(solution)/shard_map/scatter | solution.py:33
  26.0 0.0 copy-start.8
  26.0 68.0 %all_to_all.20 = bf16[32,40,896]{2,1,0:T(8,128)(2,1)S(1)} all-to-all(bf16[32,40,896]{2,1,0:T(8,128)(2,1)} %bitcast.68), channel_id=1, replica_groups=mesh['dp'=8,'expert'=32] {'expert'}, dimensions={0} | all-to-all | bytes 4587520 | tf_op jit(solution)/shard_map/all_to_all | solution.py:38
  94.0 0.0 copy-start.3
  94.0 1.4 copy-done.3
  95.5 0.0 copy-done.8
  95.5 4.6 fusion.9
  100.1 0.0 copy-start.6
  100.1 0.0 copy-start.7
  100.1 0.0 all-gather.6.cloned.1.call-update
  100.1 0.0 reduce-scatter.2.cloned.1.call-start
  100.2 0.9 copy-done.6
  101.1 0.0 copy-done.7
  101.1 0.1 copy.19
  101.2 0.1 mul.70
  101.3 7.3 %scatter_custom_fusion.1 = bf16[1280,896]{1,0:T(8,128)(2,1)} fusion(s32[1024]{0:T(1024)S(1)} %bitcast.79, f32[128,896]{1,0:T(8,128)S(1)} %convert_element_type.59, f32[1024]{0:T(1024)S(1)} %mul.70, bf16[]{:T(256)} %constant.9.clone.1), kind=kCustom, calls=%fused_computation.13 | custom fusion | flops 1835008 | bytes 2756610 | tf_op jit(solution)/shard_map/scatter | solution.py:35
  108.5 59.7 %all_to_all.21 = bf16[32,40,896]{2,1,0:T(8,128)(2,1)S(1)} all-to-all(bf16[32,40,896]{2,1,0:T(8,128)(2,1)} %bitcast.67), channel_id=1, replica_groups=mesh['dp'=8,'expert'=32] {'expert'}, dimensions={0} | all-to-all | bytes 4587520 | tf_op jit(solution)/shard_map/all_to_all | solution.py:39
  168.2 0.0 copy-start.5
  168.2 1.4 copy-done.5
  169.6 0.0 copy-done
  169.6 4.7 fusion.5
  174.2 0.0 reduce-scatter.2.cloned.1.call-update
  174.3 0.2 all-gather.4.cloned.1.call-start
  174.5 114.1 %all-gather.6.cloned.1.call-done = f32[10240,1024]{1,0:T(8,128)} async-done(((f32[1280,1024]{1,0:T(8,128)}), f32[10240,1024]{1,0:T(8,128)}) %all-gather.6.cloned.1.call-update) | async-done | bytes 41943056 | tf_op jit(solution)/shard_map/all_gather | solution.py:46
  288.6 17.9 %reduce_sum.52 = f32[1280,1024]{1,0:T(8,128)} reduce(f32[8,1280,1024]{2,1,0:T(8,128)} %bitcast.66, f32[]{:T(128)} %constant.13.clone.1), dimensions={0}, to_apply=%region_4.5 | reduce | flops 9175040 | bytes 47185924 | tf_op jit(solution)/shard_map/reduce_sum | solution.py:45
  306.5 24.8 %reduce-scatter.2.cloned.1.call-done = f32[160,1024]{1,0:T(8,128)} async-done(((f32[1280,1024]{1,0:T(8,128)}), f32[160,1024]{1,0:T(8,128)}) %reduce-scatter.2.cloned.1.call-update) | async-done | bytes 655376 | tf_op jit(solution)/shard_map/reduce_scatter | solution.py:53
  331.3 2.2 multiply_convert_fusion.1
  333.6 0.0 all-gather.4.cloned.1.call-update
  333.6 3.9 multiply_convert_fusion
  337.5 0.0 copy-start.2
  337.5 4.1 convolution_convert_fusion.1
  341.6 0.0 copy-done.2
  341.6 9.8 %all-to-all-start.1 = ((bf16[32,40,896]{2,1,0:T(8,128)(2,1)}), bf16[32,40,896]{2,1,0:T(8,128)(2,1)S(1)}, u32[]{:S(2)}, u32[]{:S(2)}) async-start(bf16[32,40,896]{2,1,0:T(8,128)(2,1)} %bitcast.74), calls=%async_computation.1 | async-start | bytes 4587520 | tf_op jit(solution)/shard_map/all_to_all | solution.py:52
  351.4 13.2 %all-gather.4.cloned.1.call-done = bf16[1280,1024]{1,0:T(8,128)(2,1)} async-done(((bf16[160,1024]{1,0:T(8,128)(2,1)}), bf16[1280,1024]{1,0:T(8,128)(2,1)}) %all-gather.4.cloned.1.call-update) | async-done | bytes 2621456 | tf_op jit(solution)/shard_map/all_gather | solution.py:62
  364.6 6.7 %convolution_convert_fusion = bf16[1280,896]{1,0:T(8,128)(2,1)} fusion(bf16[1280,1024]{1,0:T(8,128)(2,1)} %all-gather.4.cloned.1.call-done, bf16[1,896,1024]{2,1,0:T(8,128)(2,1)} %param.10), kind=kOutput, calls=%fused_computation.11 | convolution fusion | flops 2349957120 | bytes 6750208 | tf_op jit(solution)/shard_map/dot_general | solution.py:63
  371.2 34.4 %all-to-all-done.1 = bf16[32,40,896]{2,1,0:T(8,128)(2,1)S(1)} async-done(((bf16[32,40,896]{2,1,0:T(8,128)(2,1)}), bf16[32,40,896]{2,1,0:T(8,128)(2,1)S(1)}, u32[]{:S(2)}, u32[]{:S(2)}) %all-to-all-start.1) | async-done | bytes 2293792 | tf_op jit(solution)/shard_map/all_to_all | solution.py:52
  405.6 6.8 %all-to-all-start.3 = ((bf16[32,40,896]{2,1,0:T(8,128)(2,1)}), bf16[32,40,896]{2,1,0:T(8,128)(2,1)}, u32[]{:S(2)}, u32[]{:S(2)}) async-start(bf16[32,40,896]{2,1,0:T(8,128)(2,1)} %bitcast.73), calls=%async_computation.4 | async-start | bytes 4587520 | tf_op jit(solution)/shard_map/all_to_all | solution.py:67
  412.4 6.6 %convert_bitcast_fusion = bf16[1,1024,896]{2,1,0:T(8,128)(2,1)} fusion(bf16[1280,1024]{1,0:T(8,128)(2,1)} %copy-done.2, bf16[1280,896]{1,0:T(8,128)(2,1)} %bitcast.72), kind=kOutput, calls=%fused_computation.23 | convolution fusion | flops 2349727744 | bytes 6750208 | tf_op jit(solution)/shard_map/dot_general | solution.py:68
  419.0 5.2 %gather_fusion = bf16[1024,896]{1,0:T(8,128)(2,1)} fusion(bf16[1280,896]{1,0:T(8,128)(2,1)S(1)} %bitcast.65, s32[1024]{0:T(1024)S(1)} %broadcast_clamp_fusion), kind=kCustom, calls=%fused_computation | custom fusion | bytes 3674112 | tf_op jit(solution)/shard_map/gather | solution.py:75
  424.3 0.0 copy-start.4
  424.3 3.9 fusion.1
  428.1 24.7 %psum.7 = f32[128,8]{1,0:T(8,128)S(1)} all-reduce(f32[128,8]{1,0:T(8,128)S(1)} %get-tuple-element.10), channel_id=1, replica_groups=mesh['dp'=8,'expert'=32] {'dp'}, use_global_device_ids=true, to_apply=%region_10.11 | all-reduce | flops 1024 | bytes 8192 | tf_op jit(solution)/shard_map/psum | solution.py:81
  452.8 0.7 copy.26
  453.5 0.0 copy-done.4
  453.5 5.5 %convert_bitcast_fusion.1 = bf16[1,896,1024]{2,1,0:T(8,128)(2,1)} fusion(bf16[1280,896]{1,0:T(8,128)(2,1)S(1)} %bitcast.70, bf16[1280,1024]{1,0:T(8,128)(2,1)} %all-gather.4.cloned.1.call-done), kind=kOutput, calls=%fused_computation.24 | convolution fusion | flops 2349727744 | bytes 6750208 | tf_op jit(solution)/shard_map/dot_general | solution.py:71
  459.0 8.0 %all-to-all-done.3 = bf16[32,40,896]{2,1,0:T(8,128)(2,1)} async-done(((bf16[32,40,896]{2,1,0:T(8,128)(2,1)}), bf16[32,40,896]{2,1,0:T(8,128)(2,1)}, u32[]{:S(2)}, u32[]{:S(2)}) %all-to-all-start.3) | async-done | bytes 2293792 | tf_op jit(solution)/shard_map/all_to_all | solution.py:67
  467.0 0.0 copy-start.1
  467.0 7.8 %gather_fusion.1 = bf16[1024,896]{1,0:T(8,128)(2,1)} fusion(bf16[1280,896]{1,0:T(8,128)(2,1)} %bitcast.17, s32[1024]{0:T(1024)S(1)} %broadcast_clamp_fusion), kind=kCustom, calls=%fused_computation.1 | custom fusion | bytes 3674112 | tf_op jit(solution)/shard_map/gather | solution.py:83
  474.8 3.4 bitcast_reduce_fusion
  478.2 0.0 copy-done.1
  (7 shorter events, 0.1 us)
Async XLA Ops:
  7.2 162.4 %copy-start = (bf16[1,1024,896]{2,1,0:T(8,128)(2,1)S(1)}, bf16[1,1024,896]{2,1,0:T(8,128)(2,1)}, u32[]{:S(2)}) copy-start(bf16[1,1024,896]{2,1,0:T(8,128)(2,1)} %param.11) | copy-start | bytes 5505028
  7.2 281.4 %all-gather.6.cloned.1.call-start = ((), (), s32[]{:S(2)}) async-start(), calls=%async_computation.7 | async-start | bytes 47185920 | tf_op jit(solution)/shard_map/all_gather | solution.py:46
  26.0 69.5 %copy-start.8 = (bf16[1,896,1024]{2,1,0:T(8,128)(2,1)S(1)}, bf16[1,896,1024]{2,1,0:T(8,128)(2,1)}, u32[]{:S(2)}) copy-start(bf16[1,896,1024]{2,1,0:T(8,128)(2,1)} %param.10) | copy-start | bytes 5505028
  94.0 1.4 copy-start.3
  100.1 0.9 copy-start.6
  100.1 1.0 copy-start.7
  100.1 231.2 %reduce-scatter.2.cloned.1.call-start = ((), (), s32[]{:S(2)}) async-start(), calls=%async_computation.5 | async-start | bytes 5898240 | tf_op jit(solution)/shard_map/reduce_scatter | solution.py:53
  168.2 1.4 copy-start.5
  174.3 190.3 %all-gather.4.cloned.1.call-start = ((), (), s32[]{:S(2)}) async-start(), calls=%async_computation.6 | async-start | bytes 2949120 | tf_op jit(solution)/shard_map/all_gather | solution.py:62
  337.5 4.1 copy-start.2
  341.6 64.0 %all-to-all-start.1 = ((bf16[32,40,896]{2,1,0:T(8,128)(2,1)}), bf16[32,40,896]{2,1,0:T(8,128)(2,1)S(1)}, u32[]{:S(2)}, u32[]{:S(2)}) async-start(bf16[32,40,896]{2,1,0:T(8,128)(2,1)} %bitcast.74), calls=%async_computation.1 | async-start | bytes 4587520 | tf_op jit(solution)/shard_map/all_to_all | solution.py:52
  405.6 61.4 %all-to-all-start.3 = ((bf16[32,40,896]{2,1,0:T(8,128)(2,1)}), bf16[32,40,896]{2,1,0:T(8,128)(2,1)}, u32[]{:S(2)}, u32[]{:S(2)}) async-start(bf16[32,40,896]{2,1,0:T(8,128)(2,1)} %bitcast.73), calls=%async_computation.4 | async-start | bytes 4587520 | tf_op jit(solution)/shard_map/all_to_all | solution.py:67
  424.3 29.2 %copy-start.4 = (bf16[32,40,896]{2,1,0:T(8,128)(2,1)S(1)}, bf16[32,40,896]{2,1,0:T(8,128)(2,1)}, u32[]{:S(2)}) copy-start(bf16[32,40,896]{2,1,0:T(8,128)(2,1)} %copy-done.3) | copy-start | bytes 6881284
  467.0 11.2 %copy-start.1 = (bf16[1,1024,896]{2,1,0:T(8,128)(2,1)S(1)}, bf16[1,1024,896]{2,1,0:T(8,128)(2,1)}, u32[]{:S(2)}) copy-start(bf16[1,1024,896]{2,1,0:T(8,128)(2,1)} %param.11) | copy-start | bytes 5505028
Sparse Core Ops, SparseCore 0:
  100.2 188.2 all-gather.5
  291.1 40.1 reduce-scatter.1
  333.7 30.7 all-gather.3
